TPU v7x, 32 devices: a whole 2x2x4 slice. The times are simulated.
32 devices in a mesh: rep: 8 (over y, x, core), grp: 4 (over z).
Axes of the slice: x: 2, y: 2, z: 4, core: 2. Of those that a mesh axis runs over, the one named last changes fastest.
Arguments:
- images: bfloat16 [32, 577, 1024], P(('rep', 'grp')), may hold values from -6 to 6
- cotangent: bfloat16 [32, 577, 1024], P(('rep', 'grp')), may hold values from -6 to 6
- ln1_gain: bfloat16 [1024], P('grp'), may hold values from 0.5 to 1.5
- ln1_shift: bfloat16 [1024], P('grp'), may hold values from -3 to 3
- qkv_weight: bfloat16 [1024, 3072], P('grp'), may hold values from -1 to 1
- qv_bias: bfloat16 [2048], P('grp'), may hold values from -3 to 3
- out_weight: bfloat16 [1024, 1024], P('grp'), may hold values from -1.5 to 1.5
- out_bias: bfloat16 [1024], P('grp'), may hold values from -3 to 3
- ln2_gain: bfloat16 [1024], P('grp'), may hold values from 0.5 to 1.5
- ln2_shift: bfloat16 [1024], P('grp'), may hold values from -3 to 3
- fc1_weight: bfloat16 [1024, 4096], P('grp'), may hold values from -0.1875 to 0.1875
- fc1_bias: bfloat16 [4096], P('grp'), may hold values from -3 to 3
- fc2_weight: bfloat16 [4096, 1024], P('grp'), may hold values from -0.09375 to 0.09375
- fc2_bias: bfloat16 [1024], P('grp'), may hold values from -3 to 3
Outputs:
- outputs: bfloat16 [32, 577, 1024], P(('rep', 'grp'))
- input_grad: bfloat16 [32, 577, 1024], P(('rep', 'grp'))
- grad_ln1_gain: float32 [1024], P('grp')
- grad_ln1_shift: float32 [1024], P('grp')
- grad_qkv_weight: float32 [1024, 3072], P('grp')
- grad_qv_bias: float32 [2048], P('grp')
- grad_out_weight: float32 [1024, 1024], P('grp')
- grad_out_bias: float32 [1024], P('grp')
- grad_ln2_gain: float32 [1024], P('grp')
- grad_ln2_shift: float32 [1024], P('grp')
- grad_fc1_weight: float32 [1024, 4096], P('grp')
- grad_fc1_bias: float32 [4096], P('grp')
- grad_fc2_weight: float32 [4096, 1024], P('grp')
- grad_fc2_bias: float32 [1024], P('grp')
All inputs are finite; a program needn't handle non-finite values.
Results may differ from a plain program's by a relative error of at most 0.012.
Values may be sent and summed in bfloat16 or wider, within the bound.
No kernel may reach another device: no remote copies, remote signals or barrier semaphores. Data moves between devices by JAX's collectives and lax.ppermute only.
A program may use at most 256 MiB of HBM per device.

v0:
```python
import math
import jax
import jax.numpy as jnp
from jax import lax
from jax.sharding import PartitionSpec as P

H = 16
HD = 64
root_half = 0.7071067811865476
inv_root_tau = 0.3989422804014327


def norm_forward(values, gain_vec, shift_vec):
    row_mean = jnp.mean(values, axis=-1, keepdims=True)
    centred = values - row_mean
    inv_std = lax.rsqrt(jnp.mean(centred * centred, axis=-1, keepdims=True) + 1e-06)
    normed = centred * inv_std
    return (normed * gain_vec + shift_vec, normed, inv_std)


def norm_backward(grad_out, normed, inv_std, gain_vec):
    grad_hat = grad_out * gain_vec
    grad_in = inv_std * (
        grad_hat
        - jnp.mean(grad_hat, axis=-1, keepdims=True)
        - normed * jnp.mean(grad_hat * normed, axis=-1, keepdims=True)
    )
    return (grad_in, jnp.sum(grad_out * normed, axis=0), jnp.sum(grad_out, axis=0))


def split_heads(matrix):
    return matrix.reshape(matrix.shape[0], H, HD).transpose(1, 0, 2)


def join_heads(tensor):
    return tensor.transpose(1, 0, 2).reshape(tensor.shape[1], H * HD)


def grouped(tensor):
    group_size = math.gcd(H, 4)
    return tensor.reshape((H // group_size, group_size) + tensor.shape[1:])


def ungrouped(tensor):
    return tensor.reshape((H,) + tensor.shape[2:])


def head_scores(query_group, key_group):
    return jnp.einsum("hqd,hkd->hqk", query_group, key_group, preferred_element_type=jnp.float32)


def attend_group(group):
    query_group, key_group, value_group = group
    scores = head_scores(query_group, key_group)
    row_max = jnp.max(scores, axis=-1, keepdims=True)
    log_total = row_max + jnp.log(jnp.sum(jnp.exp(scores - row_max), axis=-1, keepdims=True))
    probs = jnp.exp(scores - log_total).astype(jnp.bfloat16)
    mixed = jnp.einsum("hqk,hkd->hqd", probs, value_group, preferred_element_type=jnp.float32)
    return (mixed, log_total)


def attend_back(group):
    query_group, key_group, value_group, log_total, grad_mixed = group
    probs_exact = jnp.exp(head_scores(query_group, key_group) - log_total)
    grad_probs = jnp.einsum(
        "hqd,hkd->hqk", grad_mixed, value_group, preferred_element_type=jnp.float32
    )
    row_dot = jnp.sum(probs_exact * grad_probs, axis=-1, keepdims=True)
    grad_scores = (probs_exact * (grad_probs - row_dot)).astype(jnp.bfloat16)
    grad_query = (
        jnp.einsum("hqk,hkd->hqd", grad_scores, key_group, preferred_element_type=jnp.float32)
        * 0.125
    )
    grad_key = jnp.einsum(
        "hqk,hqd->hkd", grad_scores, query_group, preferred_element_type=jnp.float32
    )
    grad_value = jnp.einsum(
        "hqk,hqd->hkd",
        probs_exact.astype(jnp.bfloat16),
        grad_mixed,
        preferred_element_type=jnp.float32,
    )
    return (grad_query, grad_key, grad_value)


def forward_image(image, params):
    (
        gain_first,
        shift_first,
        attn_in,
        bias_pair,
        attn_out,
        bias_attn,
        gain_second,
        shift_second,
        mlp_up,
        bias_up,
        mlp_down,
        bias_down,
    ) = params
    model_width = attn_out.shape[0]
    incoming = image.astype(jnp.float32)
    normed_f, normed_one, inv_std_one = norm_forward(
        incoming, gain_first.astype(jnp.float32), shift_first.astype(jnp.float32)
    )
    normed_in = normed_f.astype(jnp.bfloat16)
    projected = jnp.dot(normed_in, attn_in, preferred_element_type=jnp.float32)
    bias_float = bias_pair.astype(jnp.float32)
    query_heads = split_heads(
        ((projected[:, :model_width] + bias_float[:model_width]) * 0.125).astype(jnp.bfloat16)
    )
    key_heads = split_heads(projected[:, model_width : 2 * model_width].astype(jnp.bfloat16))
    value_heads = split_heads(
        (projected[:, 2 * model_width :] + bias_float[model_width:]).astype(jnp.bfloat16)
    )
    mixed, log_total = lax.map(
        attend_group, (grouped(query_heads), grouped(key_heads), grouped(value_heads))
    )
    attended = join_heads(ungrouped(mixed)).astype(jnp.bfloat16)
    residual = (
        incoming
        + jnp.dot(attended, attn_out, preferred_element_type=jnp.float32)
        + bias_attn.astype(jnp.float32)
    )
    mid_f, normed_two, inv_std_two = norm_forward(
        residual, gain_second.astype(jnp.float32), shift_second.astype(jnp.float32)
    )
    normed_mid = mid_f.astype(jnp.bfloat16)
    pre_act = jnp.dot(normed_mid, mlp_up, preferred_element_type=jnp.float32) + bias_up.astype(
        jnp.float32
    )
    normal_cdf = 0.5 * (1.0 + lax.erf(pre_act * root_half))
    activated = (pre_act * normal_cdf).astype(jnp.bfloat16)
    block_out = (
        residual
        + jnp.dot(activated, mlp_down, preferred_element_type=jnp.float32)
        + bias_down.astype(jnp.float32)
    ).astype(jnp.bfloat16)
    stored = (
        normed_in,
        normed_one,
        inv_std_one,
        query_heads,
        key_heads,
        value_heads,
        ungrouped(log_total),
        attended,
        normed_mid,
        normed_two,
        inv_std_two,
        pre_act,
        normal_cdf,
        activated,
    )
    return (block_out, stored)


def backward_image(grad_block, stored, params):
    (
        gain_first,
        shift_first,
        attn_in,
        bias_pair,
        attn_out,
        bias_attn,
        gain_second,
        shift_second,
        mlp_up,
        bias_up,
        mlp_down,
        bias_down,
    ) = params
    (
        normed_in,
        normed_one,
        inv_std_one,
        query_heads,
        key_heads,
        value_heads,
        log_total,
        attended,
        normed_mid,
        normed_two,
        inv_std_two,
        pre_act,
        normal_cdf,
        activated,
    ) = stored
    grad_top = grad_block.astype(jnp.float32)
    grad_down = jnp.dot(activated.T, grad_block, preferred_element_type=jnp.float32)
    grad_bias_down = jnp.sum(grad_top, axis=0)
    grad_hidden = jnp.dot(grad_block, mlp_down.T, preferred_element_type=jnp.float32)
    density = jnp.exp(-0.5 * pre_act * pre_act) * inv_root_tau
    grad_pre = grad_hidden * (normal_cdf + pre_act * density)
    grad_pre_b = grad_pre.astype(jnp.bfloat16)
    grad_up = jnp.dot(normed_mid.T, grad_pre_b, preferred_element_type=jnp.float32)
    grad_bias_up = jnp.sum(grad_pre, axis=0)
    grad_mid = jnp.dot(grad_pre_b, mlp_up.T, preferred_element_type=jnp.float32)
    grad_norm_mid, grad_gain_second, grad_shift_second = norm_backward(
        grad_mid, normed_two, inv_std_two, gain_second.astype(jnp.float32)
    )
    grad_residual = grad_top + grad_norm_mid
    grad_bias_attn = jnp.sum(grad_residual, axis=0)
    grad_res_b = grad_residual.astype(jnp.bfloat16)
    grad_attn_out = jnp.dot(attended.T, grad_res_b, preferred_element_type=jnp.float32)
    grad_attended = split_heads(
        jnp.dot(grad_res_b, attn_out.T, preferred_element_type=jnp.float32).astype(jnp.bfloat16)
    )
    grad_query, grad_key, grad_value = lax.map(
        attend_back,
        (
            grouped(query_heads),
            grouped(key_heads),
            grouped(value_heads),
            grouped(log_total),
            grouped(grad_attended),
        ),
    )
    grad_query = join_heads(ungrouped(grad_query))
    grad_key = join_heads(ungrouped(grad_key))
    grad_value = join_heads(ungrouped(grad_value))
    grad_projected = jnp.concatenate([grad_query, grad_key, grad_value], axis=1)
    grad_bias_pair = jnp.concatenate([jnp.sum(grad_query, axis=0), jnp.sum(grad_value, axis=0)])
    grad_proj_b = grad_projected.astype(jnp.bfloat16)
    grad_attn_in = jnp.dot(normed_in.T, grad_proj_b, preferred_element_type=jnp.float32)
    grad_in_norm = jnp.dot(grad_proj_b, attn_in.T, preferred_element_type=jnp.float32)
    grad_norm_in, grad_gain_first, grad_shift_first = norm_backward(
        grad_in_norm, normed_one, inv_std_one, gain_first.astype(jnp.float32)
    )
    input_grad = (grad_residual + grad_norm_in).astype(jnp.bfloat16)
    grads = (
        grad_gain_first,
        grad_shift_first,
        grad_attn_in,
        grad_bias_pair,
        grad_attn_out,
        grad_bias_attn,
        grad_gain_second,
        grad_shift_second,
        grad_up,
        grad_bias_up,
        grad_down,
        grad_bias_down,
    )
    return (input_grad, grads)


def on_device(
    images,
    cotangent,
    ln1_gain,
    ln1_shift,
    qkv_weight,
    qv_bias,
    out_weight,
    out_bias,
    ln2_gain,
    ln2_shift,
    fc1_weight,
    fc1_bias,
    fc2_weight,
    fc2_bias,
):
    gathered = (
        lax.all_gather(ln1_gain, "grp", axis=0, tiled=True),
        lax.all_gather(ln1_shift, "grp", axis=0, tiled=True),
        lax.all_gather(qkv_weight, "grp", axis=0, tiled=True),
        lax.all_gather(qv_bias, "grp", axis=0, tiled=True),
        lax.all_gather(out_weight, "grp", axis=0, tiled=True),
        lax.all_gather(out_bias, "grp", axis=0, tiled=True),
        lax.all_gather(ln2_gain, "grp", axis=0, tiled=True),
        lax.all_gather(ln2_shift, "grp", axis=0, tiled=True),
        lax.all_gather(fc1_weight, "grp", axis=0, tiled=True),
        lax.all_gather(fc1_bias, "grp", axis=0, tiled=True),
        lax.all_gather(fc2_weight, "grp", axis=0, tiled=True),
        lax.all_gather(fc2_bias, "grp", axis=0, tiled=True),
    )
    position = 0
    block_out, stored = forward_image(images[position], gathered)
    block_outs = [block_out]
    stored_list = [stored]
    regathered = (
        lax.all_gather(ln1_gain, "grp", axis=0, tiled=True),
        lax.all_gather(ln1_shift, "grp", axis=0, tiled=True),
        lax.all_gather(qkv_weight, "grp", axis=0, tiled=True),
        lax.all_gather(qv_bias, "grp", axis=0, tiled=True),
        lax.all_gather(out_weight, "grp", axis=0, tiled=True),
        lax.all_gather(out_bias, "grp", axis=0, tiled=True),
        lax.all_gather(ln2_gain, "grp", axis=0, tiled=True),
        lax.all_gather(ln2_shift, "grp", axis=0, tiled=True),
        lax.all_gather(fc1_weight, "grp", axis=0, tiled=True),
        lax.all_gather(fc1_bias, "grp", axis=0, tiled=True),
        lax.all_gather(fc2_weight, "grp", axis=0, tiled=True),
        lax.all_gather(fc2_bias, "grp", axis=0, tiled=True),
    )
    position = 0
    input_grad, grads = backward_image(cotangent[position], stored_list[position], regathered)
    input_grads = [input_grad]
    shares = (
        lax.psum_scatter(grads[0], "grp", scatter_dimension=0, tiled=True),
        lax.psum_scatter(grads[1], "grp", scatter_dimension=0, tiled=True),
        lax.psum_scatter(grads[2], "grp", scatter_dimension=0, tiled=True),
        lax.psum_scatter(grads[3], "grp", scatter_dimension=0, tiled=True),
        lax.psum_scatter(grads[4], "grp", scatter_dimension=0, tiled=True),
        lax.psum_scatter(grads[5], "grp", scatter_dimension=0, tiled=True),
        lax.psum_scatter(grads[6], "grp", scatter_dimension=0, tiled=True),
        lax.psum_scatter(grads[7], "grp", scatter_dimension=0, tiled=True),
        lax.psum_scatter(grads[8], "grp", scatter_dimension=0, tiled=True),
        lax.psum_scatter(grads[9], "grp", scatter_dimension=0, tiled=True),
        lax.psum_scatter(grads[10], "grp", scatter_dimension=0, tiled=True),
        lax.psum_scatter(grads[11], "grp", scatter_dimension=0, tiled=True),
    )
    owned_parts = lax.psum(
        (
            shares[0],
            shares[1],
            shares[2],
            shares[3],
            shares[4],
            shares[5],
            shares[6],
            shares[7],
            shares[8],
            shares[9],
            shares[10],
            shares[11],
        ),
        "rep",
    )
    return (
        jnp.stack(block_outs),
        jnp.stack(input_grads),
        owned_parts[0],
        owned_parts[1],
        owned_parts[2],
        owned_parts[3],
        owned_parts[4],
        owned_parts[5],
        owned_parts[6],
        owned_parts[7],
        owned_parts[8],
        owned_parts[9],
        owned_parts[10],
        owned_parts[11],
    )


def solution(mesh):
    return jax.shard_map(
        on_device,
        mesh=mesh,
        in_specs=(
            P(("rep", "grp"), None, None),
            P(("rep", "grp"), None, None),
            P("grp"),
            P("grp"),
            P("grp", None),
            P("grp"),
            P("grp", None),
            P("grp"),
            P("grp"),
            P("grp"),
            P("grp", None),
            P("grp"),
            P("grp", None),
            P("grp"),
        ),
        out_specs=(
            P(("rep", "grp"), None, None),
            P(("rep", "grp"), None, None),
            P("grp"),
            P("grp"),
            P("grp", None),
            P("grp"),
            P("grp", None),
            P("grp"),
            P("grp"),
            P("grp"),
            P("grp", None),
            P("grp"),
            P("grp", None),
            P("grp"),
        ),
        check_vma=False,
    )
```

profile of v0, /device:TPU:0, one launch (start us, length us, event | category | flops | bytes accessed | tf_op | source)
XLA Modules:
  0.0 1556.5 jit_solution(15243761869660950640)
XLA Ops:
  10.2 12.8 all-gather.3
  32.3 12.8 all-gather
  45.1 17.2 %all_gather.51 = bf16[4096]{0:T(1024)(128)(2,1)S(1)} all-gather(bf16[1024]{0:T(1024)(128)(2,1)S(1)} %copy-done.30), channel_id=1, replica_groups=mesh['rep'=8,'grp'=4] {'grp'}, dimensions={0}, use_global_device_ids=true | all-gather | bytes 10240 | tf_op jit(solution)/shard_map/all_gather | solution.py:274
  70.6 17.1 %all-gather.4 = bf16[4,1,256]{2,1,0:T(2,128)(2,1)S(1)} all-gather(bf16[1,1,256]{2,1,0:T(2,128)(2,1)S(1)} %reshape.182), channel_id=1, replica_groups=mesh['rep'=8,'grp'=4] {'grp'}, dimensions={0}, use_global_device_ids=true | all-gather | bytes 2560 | tf_op jit(solution)/shard_map/all_gather | solution.py:271
  87.7 17.2 %all-gather.2 = bf16[4,1,512]{2,1,0:T(2,128)(2,1)S(1)} all-gather(bf16[1,1,512]{2,1,0:T(2,128)(2,1)S(1)} %reshape.178), channel_id=1, replica_groups=mesh['rep'=8,'grp'=4] {'grp'}, dimensions={0}, use_global_device_ids=true | all-gather | bytes 5120 | tf_op jit(solution)/shard_map/all_gather | solution.py:268
  105.7 22.4 %all-gather.12.cloned.1.call-done = bf16[1024,3072]{1,0:T(8,128)(2,1)} async-done(((bf16[256,3072]{1,0:T(8,128)(2,1)}), bf16[1024,3072]{1,0:T(8,128)(2,1)}) %all-gather.12.cloned.1.call-update) | async-done | bytes 6291472 | tf_op jit(solution)/shard_map/all_gather | solution.py:267
  142.4 22.3 %while.28 = (s32[]{:T(128)}, bf16[4,4,577,64]{2,3,1,0:T(8,128)(2,1)}, f32[4,4,577,1]{2,1,3,0:T(4,128)S(1)}, bf16[4,4,577,64]{2,3,1,0:T(8,128)(2,1)S(1)}, bf16[4,...) while((s32[]{:T(128)}, bf16[4,4,577,64]{2,3,1,0:T(8,128)(2,1)}, ...), condition=%wide.region_5.6_spmd.clone, body=%wide.region_2.5_spmd.sunk.clone | while | flops 347575552 | bytes 27806936 | solution.py:116
  179.3 144.3 %all-gather.16.cloned.1.call-done = bf16[1024,4096]{1,0:T(8,128)(2,1)} async-done(((bf16[256,4096]{1,0:T(8,128)(2,1)}), bf16[1024,4096]{1,0:T(8,128)(2,1)}) %all-gather.16.cloned.1.call-update) | async-done | bytes 8388624 | tf_op jit(solution)/shard_map/all_gather | solution.py:273
  323.6 12.6 multiply_convert_fusion.1
  336.1 136.7 %all-gather.18.cloned.1.call-done = bf16[4096,1024]{1,0:T(8,128)(2,1)} async-done(((bf16[1024,1024]{1,0:T(8,128)(2,1)}), bf16[4096,1024]{1,0:T(8,128)(2,1)}) %all-gather.18.cloned.1.call-update) | async-done | bytes 8388624 | tf_op jit(solution)/shard_map/all_gather | solution.py:275
  472.8 12.5 fusion.98
  504.9 37.4 %while.29 = (s32[]{:T(128)}, f32[4,4,577,64]{2,3,1,0:T(8,128)}, bf16[4,4,577,64]{2,3,1,0:T(8,128)(2,1)}, f32[4,4,577,64]{2,3,1,0:T(8,128)}, bf16[4,4,577,64]{2,3...) while((s32[]{:T(128)}, f32[4,4,577,64]{2,3,1,0:T(8,128)}, ...), condition=%wide.region_12.13_spmd.clone, body=%wide.region_10.12_spmd.sunk.clone | while | flops 864429056 | bytes 60423508 | solution.py:209
  547.1 11.5 fusion.77
  560.3 13.3 fusion.73
  573.6 12.3 fusion.81
  586.0 208.6 %reduce-scatter.5.cloned.1.call-done = f32[256,3072]{1,0:T(8,128)} async-done(((f32[1024,3072]{1,0:T(8,128)}), f32[256,3072]{1,0:T(8,128)}) %reduce-scatter.5.cloned.1.call-update) | async-done | bytes 3145744 | tf_op jit(solution)/shard_map/reduce_scatter | solution.py:302
  794.6 283.9 %reduce-scatter.9.cloned.1.call-done = f32[256,4096]{1,0:T(8,128)} async-done(((f32[1024,4096]{1,0:T(8,128)}), f32[256,4096]{1,0:T(8,128)}) %reduce-scatter.9.cloned.1.call-update) | async-done | bytes 4194320 | tf_op jit(solution)/shard_map/reduce_scatter | solution.py:308
  1078.5 283.5 %reduce-scatter.11.cloned.1.call-done = f32[1024,1024]{1,0:T(8,128)} async-done(((f32[4096,1024]{1,0:T(8,128)}), f32[1024,1024]{1,0:T(8,128)}) %reduce-scatter.11.cloned.1.call-update) | async-done | bytes 4194320 | tf_op jit(solution)/shard_map/reduce_scatter | solution.py:310
  1362.6 10.5 all-gather.6
  1379.8 10.5 fusion.67
  1390.3 16.5 %all-reduce.10 = (f32[1024]{0:T(1024)S(1)}, f32[1024]{0:T(1024)S(1)}, f32[2048]{0:T(1024)S(1)}, f32[1024]{0:T(1024)S(1)}, f32[1024]{0:T(1024)S(1)}, /*index=5*/f...) all-reduce(f32[1024]{0:T(1024)S(1)} %get-tuple-element.103, ...), channel_id=2, replica_groups=mesh['rep'=8,'grp'=4] {'grp'}, use_global_device_ids=true, to_apply=%region_16.17.clone | all-reduce | flops 12288 | bytes 98304
  1407.3 23.6 %all-reduce.8 = (f32[256]{0:T(256)}, f32[256]{0:T(256)}, f32[512]{0:T(512)}, f32[256]{0:T(256)}, f32[256]{0:T(256)}, /*index=5*/f32[256]{0:T(256)}, f32[1024]{0:T(1024)}, f32[256]{0:T(256)}) all-reduce(f32[256]{0:T(256)S(1)} %dynamic-slice.1, f32[256]{0:T(256)S(1)} %dynamic-slice.3, ...), channel_id=1, replica_groups=mesh['rep'=8,'grp'=4] {'rep'}, use_global_device_ids=true, to_apply=%region_17.18 | all-reduce | flops 3072 | bytes 24576 | tf_op jit(solution)/shard_map/psum | solution.py:313
  1436.5 9.7 fusion.79
  1446.3 92.8 %all-reduce.13.cloned.1.call-done = (f32[256,3072]{1,0:T(8,128)}, f32[256,1024]{1,0:T(8,128)}, f32[256,4096]{1,0:T(8,128)}, f32[1024,1024]{1,0:T(8,128)}) async-done(((f32[256,3072]{1,0:T(8,128)}, f32[256,1024]{1,0:T(8,128)}, f32[256,4096]{1,0:T(8,128)}, f32[1024,1024]{1,0:T(8,128)}), (f32[256,3072]{1,0:T(8,128)}, f32[256,1024]{1,0:T(8,128)}, f32[256,4096]{1,0:T(8,128)}, ...) | async-done | bytes 12582928 | tf_op jit(solution)/shard_map/psum | solution.py:313
  (239 shorter events, 157.3 us)
Async XLA Ops:
  7.2 120.9 %all-gather.12.cloned.1.call-start = ((), (), s32[]{:S(2)}) async-start(), calls=%async_computation.4 | async-start | bytes 7864320 | tf_op jit(solution)/shard_map/all_gather | solution.py:267
  7.9 165.6 %all-gather.14.cloned.1.call-start = ((), (), s32[]{:S(2)}) async-start(), calls=%async_computation.5 | async-start | bytes 2621440 | tf_op jit(solution)/shard_map/all_gather | solution.py:269
  8.7 314.9 %all-gather.16.cloned.1.call-start = ((), (), s32[]{:S(2)}) async-start(), calls=%async_computation.6 | async-start | bytes 10485760 | tf_op jit(solution)/shard_map/all_gather | solution.py:273
  9.4 463.4 %all-gather.18.cloned.1.call-start = ((), (), s32[]{:S(2)}) async-start(), calls=%async_computation.7 | async-start | bytes 10485760 | tf_op jit(solution)/shard_map/all_gather | solution.py:275
  10.0 14.2 copy-start.34
  10.0 22.2 %copy-start.35 = (bf16[256]{0:T(256)(128)(2,1)S(1)}, bf16[256]{0:T(256)(128)(2,1)}, u32[]{:S(2)}) copy-start(bf16[256]{0:T(256)(128)(2,1)} %param.20) | copy-start | bytes 1540
  10.0 35.1 %copy-start.31 = (bf16[512]{0:T(512)(128)(2,1)S(1)}, bf16[512]{0:T(512)(128)(2,1)}, u32[]{:S(2)}) copy-start(bf16[512]{0:T(512)(128)(2,1)} %param.23) | copy-start | bytes 3076
  10.0 35.1 %copy-start.30 = (bf16[1024]{0:T(1024)(128)(2,1)S(1)}, bf16[1024]{0:T(1024)(128)(2,1)}, u32[]{:S(2)}) copy-start(bf16[1024]{0:T(1024)(128)(2,1)} %param.29) | copy-start | bytes 6148
  10.0 52.3 %copy-start.36 = (bf16[256]{0:T(256)(128)(2,1)S(1)}, bf16[256]{0:T(256)(128)(2,1)}, u32[]{:S(2)}) copy-start(bf16[256]{0:T(256)(128)(2,1)} %param.27) | copy-start | bytes 1540
  10.0 60.5 %copy-start.37 = (bf16[256]{0:T(256)(128)(2,1)S(1)}, bf16[256]{0:T(256)(128)(2,1)}, u32[]{:S(2)}) copy-start(bf16[256]{0:T(256)(128)(2,1)} %param.26) | copy-start | bytes 1540
  10.0 94.8 %copy-start.4 = (bf16[1,577,1024]{2,1,0:T(8,128)(2,1)S(1)}, bf16[1,577,1024]{2,1,0:T(8,128)(2,1)}, u32[]{:S(2)}) copy-start(bf16[1,577,1024]{2,1,0:T(8,128)(2,1)} %param.18) | copy-start | bytes 3545092
  10.1 576.0 %reduce-scatter.7.cloned.1.call-start = ((), (), s32[]{:S(2)}) async-start(), calls=%async_computation.9 | async-start | bytes 5242880 | tf_op jit(solution)/shard_map/reduce_scatter | solution.py:304
  23.1 82.5 %copy-start.8 = (bf16[4,4,577,64]{2,3,1,0:T(8,128)(2,1)}, bf16[4,4,577,64]{2,3,1,0:T(8,128)(2,1)S(1)}, u32[]{:S(2)}) copy-start(bf16[4,4,577,64]{2,3,1,0:T(8,128)(2,1)S(1)} %fusion.95) | copy-start | bytes 3545092
  32.2 102.4 %copy-start.28 = (f32[4,1,256]{2,1,0:T(1,128)}, f32[4,1,256]{2,1,0:T(1,128)S(1)}, u32[]{:S(2)}) copy-start(f32[4,1,256]{2,1,0:T(1,128)S(1)} %convert_element_type.114) | copy-start | bytes 12292
  45.1 89.5 %copy-start.24 = (f32[4,1,256]{2,1,0:T(1,128)}, f32[4,1,256]{2,1,0:T(1,128)S(1)}, u32[]{:S(2)}) copy-start(f32[4,1,256]{2,1,0:T(1,128)S(1)} %convert_element_type.113) | copy-start | bytes 12292
  105.1 29.5 %copy-start.22 = (f32[577]{0:T(1024)}, f32[577]{0:T(1024)S(1)}, u32[]{:S(2)}) copy-start(f32[577]{0:T(1024)S(1)} %broadcast_multiply_fusion.5) | copy-start | bytes 6928
  105.6 29.0 %copy-start.26 = (f32[577]{0:T(1024)}, f32[577]{0:T(1024)S(1)}, u32[]{:S(2)}) copy-start(f32[577]{0:T(1024)S(1)} %add_rsqrt_fusion.1) | copy-start | bytes 6928
  472.8 12.5 copy-start.1
  472.8 12.5 copy-start.32
  504.8 289.8 %reduce-scatter.5.cloned.1.call-start = ((), (), s32[]{:S(2)}) async-start(), calls=%async_computation.8 | async-start | bytes 15728640 | tf_op jit(solution)/shard_map/reduce_scatter | solution.py:302
  558.6 519.9 %reduce-scatter.9.cloned.1.call-start = ((), (), s32[]{:S(2)}) async-start(), calls=%async_computation.10 | async-start | bytes 20971520 | tf_op jit(solution)/shard_map/reduce_scatter | solution.py:308
  573.6 788.4 %reduce-scatter.11.cloned.1.call-start = ((), (), s32[]{:S(2)}) async-start(), calls=%async_computation.11 | async-start | bytes 20971520 | tf_op jit(solution)/shard_map/reduce_scatter | solution.py:310
  585.9 953.1 %all-reduce.13.cloned.1.call-start = ((), (), s32[]{:S(2)}) async-start(), calls=%async_computation.12 | async-start | bytes 25165824 | tf_op jit(solution)/shard_map/psum | solution.py:313
  1361.9 11.1 copy-start.39
  (40 other events, 83.5 us)
Sparse Core Ops, SparseCore 0:
  9.6 118.4 all-gather.11
  129.6 43.8 all-gather.13
  175.1 148.4 all-gather.15
  325.0 147.7 all-gather.17
  505.0 74.9 reduce-scatter.6
  582.2 212.3 reduce-scatter.4
  797.0 281.4 reduce-scatter.8
  1080.8 281.0 reduce-scatter.10
  1365.9 173.1 all-reduce.12
where the time goes:
time: 1570 us; the launch traced here: 1560 us
  waiting for transfers between devices  1180 us (75%)
  matrix products  151 us (10%)
  blocking collectives  144 us (9%)
  local copies, waits for them, and re-layouts  35.9 us (2%)
  other arithmetic  24.6 us (2%)
  between operations  16.5 us (1%)
    reduce_scatter x1, waiting for transfers between devices, on_device(): lax.psum_scatter(grads[8], 'grp', scatter_dimension=0, tiled=True)  284 us
    reduce_scatter x1, waiting for transfers between devices, on_device(): lax.psum_scatter(grads[10], 'grp', scatter_dimension=0, tiled=True)  283 us
    reduce_scatter x1, waiting for transfers between devices, on_device(): lax.psum_scatter(grads[2], 'grp', scatter_dimension=0, tiled=True)  209 us
    all_gather x1, waiting for transfers between devices, on_device(): lax.all_gather(fc1_weight, 'grp', axis=0, tiled=True)  144 us
    all_gather x1, waiting for transfers between devices, on_device(): lax.all_gather(fc2_weight, 'grp', axis=0, tiled=True)  137 us
    psum x1, waiting for transfers between devices, on_device(): lax.psum((shares[0], shares[1], shares[2], shares[3], shares[4], shares[5...  92.8 us
  transfers between devices with their start and end apart: 9, of which 8 were waited for; matrix products, arithmetic and copies ran while one was open for 10% of the time, Pallas kernels for 0%

commit v1 on v0

--- a/solution.py
+++ b/solution.py
@@ -8,6 +8,27 @@
 HD = 64
 root_half = 0.7071067811865476
 inv_root_tau = 0.3989422804014327
+
+
+def ring_gather(x, axis, dim):
+    devices, here, rows = (lax.axis_size(axis), lax.axis_index(axis), x.shape[dim])
+    right = [(i, (i + 1) % devices) for i in range(devices)]
+    downward = [(i, (i - 1) % devices) for i in range(devices)]
+    result = jnp.zeros((*x.shape[:dim], devices * rows, *x.shape[dim + 1 :]), x.dtype)
+    result = lax.dynamic_update_slice_in_dim(result, x, here * rows, axis=dim)
+    from_left = from_right = x
+    halfway = devices // 2
+    for step in range(1, halfway + 1):
+        from_left = lax.ppermute(from_left, axis, right)
+        result = lax.dynamic_update_slice_in_dim(
+            result, from_left, (here - step) % devices * rows, axis=dim
+        )
+        if step < devices - halfway:
+            from_right = lax.ppermute(from_right, axis, downward)
+            result = lax.dynamic_update_slice_in_dim(
+                result, from_right, (here + step) % devices * rows, axis=dim
+            )
+    return result
 
 
 def norm_forward(values, gain_vec, shift_vec):
@@ -272,7 +293,7 @@
         lax.all_gather(ln2_shift, "grp", axis=0, tiled=True),
         lax.all_gather(fc1_weight, "grp", axis=0, tiled=True),
         lax.all_gather(fc1_bias, "grp", axis=0, tiled=True),
-        lax.all_gather(fc2_weight, "grp", axis=0, tiled=True),
+        ring_gather(fc2_weight, "grp", 0),
         lax.all_gather(fc2_bias, "grp", axis=0, tiled=True),
     )
     position = 0

time: 1570 us -> 1660 us (1.057)
  blocking collectives: 144 us -> 182 us
  waiting for transfers between devices: 1180 us -> 1210 us
  local copies, waits for them, and re-layouts: 35.9 us -> 54.9 us
    reduce_scatter x1, waiting for transfers between devices: 209 us -> 289 us  [on_device(): lax.psum_scatter(grads[2], 'grp', scatter_dimension=0, tiled=True)]
    psum x1, waiting for transfers between devices: 92.8 us -> 38 us  [on_device(): lax.psum((shares[0], shares[1], shares[2], shares[3], shares[4], shares[5...]
    all_gather x1, blocking collectives: 10.5 us -> 49.1 us  [on_device(): lax.all_gather(fc2_bias, 'grp', axis=0, tiled=True)]
  transfers between devices with their start and end apart: 9 -> 12, of which waited for: 8 -> 8; matrix products, arithmetic and copies ran while one was open for 10% -> 11% of each run, Pallas kernels for 0% -> 0%
where the time goes in v1:
time: 1660 us; the launch traced here: 1650 us
  waiting for transfers between devices  1210 us (73%)
  blocking collectives  182 us (11%)
  matrix products  152 us (9%)
  local copies, waits for them, and re-layouts  54.9 us (3%)
  other arithmetic  27 us (2%)
  between operations  16.6 us (1%)
    reduce_scatter x1, waiting for transfers between devices, on_device(): lax.psum_scatter(grads[2], 'grp', scatter_dimension=0, tiled=True)  289 us
    reduce_scatter x1, waiting for transfers between devices, on_device(): lax.psum_scatter(grads[10], 'grp', scatter_dimension=0, tiled=True)  283 us
    reduce_scatter x1, waiting for transfers between devices, on_device(): lax.psum_scatter(grads[8], 'grp', scatter_dimension=0, tiled=True)  283 us
    all_gather x1, waiting for transfers between devices, on_device(): lax.all_gather(fc1_weight, 'grp', axis=0, tiled=True)  144 us
    all_gather x1, waiting for transfers between devices, on_device(): lax.all_gather(fc2_weight, 'grp', axis=0, tiled=True)  137 us
    all_gather x1, blocking collectives, on_device(): lax.all_gather(fc2_bias, 'grp', axis=0, tiled=True)  49.1 us
    psum x1, waiting for transfers between devices, on_device(): lax.psum((shares[0], shares[1], shares[2], shares[3], shares[4], shares[5...  38 us
  transfers between devices with their start and end apart: 12, of which 8 were waited for; matrix products, arithmetic and copies ran while one was open for 11% of the time, Pallas kernels for 0%

profile of v1, /device:TPU:0, one launch (start us, length us, event | category | flops | bytes accessed | tf_op | source)
XLA Modules:
  0.0 1646.6 jit_solution(7917604791493379764)
XLA Ops:
  10.2 12.8 all-gather
  33.4 11.9 all-gather.3
  53.5 18.6 %all_gather.50 = bf16[4096]{0:T(1024)(128)(2,1)S(1)} all-gather(bf16[1024]{0:T(1024)(128)(2,1)S(1)} %copy-done.31), channel_id=1, replica_groups=mesh['rep'=8,'grp'=4] {'grp'}, dimensions={0}, use_global_device_ids=true | all-gather | bytes 10240 | tf_op jit(solution)/shard_map/all_gather | solution.py:295
  72.1 15.6 all-gather.5
  87.7 17.1 %all-gather.2 = bf16[4,1,512]{2,1,0:T(2,128)(2,1)S(1)} all-gather(bf16[1,1,512]{2,1,0:T(2,128)(2,1)S(1)} %reshape.178), channel_id=1, replica_groups=mesh['rep'=8,'grp'=4] {'grp'}, dimensions={0}, use_global_device_ids=true | all-gather | bytes 5120 | tf_op jit(solution)/shard_map/all_gather | solution.py:289
  105.6 22.6 %all-gather.12.cloned.1.call-done = bf16[1024,3072]{1,0:T(8,128)(2,1)} async-done(((bf16[256,3072]{1,0:T(8,128)(2,1)}), bf16[1024,3072]{1,0:T(8,128)(2,1)}) %all-gather.12.cloned.1.call-update) | async-done | bytes 6291472 | tf_op jit(solution)/shard_map/all_gather | solution.py:288
  142.5 22.3 %while.28 = (s32[]{:T(128)}, bf16[4,4,577,64]{2,3,1,0:T(8,128)(2,1)}, f32[4,4,577,1]{2,1,3,0:T(4,128)S(1)}, bf16[4,4,577,64]{2,3,1,0:T(8,128)(2,1)S(1)}, bf16[4,...) while((s32[]{:T(128)}, bf16[4,4,577,64]{2,3,1,0:T(8,128)(2,1)}, ...), condition=%wide.region_5.6_spmd.clone, body=%wide.region_2.5_spmd.sunk.clone | while | flops 347575552 | bytes 27806928 | solution.py:137
  179.2 144.3 %all-gather.16.cloned.1.call-done = bf16[1024,4096]{1,0:T(8,128)(2,1)} async-done(((bf16[256,4096]{1,0:T(8,128)(2,1)}), bf16[1024,4096]{1,0:T(8,128)(2,1)}) %all-gather.16.cloned.1.call-update) | async-done | bytes 8388624 | tf_op jit(solution)/shard_map/all_gather | solution.py:294
  323.6 12.5 multiply_convert_fusion.1
  336.1 136.7 %all-gather.18.cloned.1.call-done = bf16[4096,1024]{1,0:T(8,128)(2,1)} async-done(((bf16[1024,1024]{1,0:T(8,128)(2,1)}), bf16[4096,1024]{1,0:T(8,128)(2,1)}) %all-gather.18.cloned.1.call-update) | async-done | bytes 8388624 | tf_op jit(solution)/shard_map/all_gather | solution.py:314
  472.8 13.1 fusion.98
  505.5 41.9 %while.29 = (s32[]{:T(128)}, f32[4,4,577,64]{2,3,1,0:T(8,128)}, bf16[4,4,577,64]{2,3,1,0:T(8,128)(2,1)}, f32[4,4,577,64]{2,3,1,0:T(8,128)}, bf16[4,4,577,64]{2,3...) while((s32[]{:T(128)}, f32[4,4,577,64]{2,3,1,0:T(8,128)}, ...), condition=%wide.region_12.13_spmd.clone, body=%wide.region_10.12_spmd.sunk.clone | while | flops 864429056 | bytes 60423500 | solution.py:230
  553.0 11.6 fusion.77
  566.2 13.3 fusion.73
  579.6 12.8 fusion.81
  596.4 288.7 %reduce-scatter.5.cloned.1.call-done = f32[256,3072]{1,0:T(8,128)} async-done(((f32[1024,3072]{1,0:T(8,128)}), f32[256,3072]{1,0:T(8,128)}) %reduce-scatter.5.cloned.1.call-update) | async-done | bytes 3145744 | tf_op jit(solution)/shard_map/reduce_scatter | solution.py:323
  885.1 283.4 %reduce-scatter.9.cloned.1.call-done = f32[256,4096]{1,0:T(8,128)} async-done(((f32[1024,4096]{1,0:T(8,128)}), f32[256,4096]{1,0:T(8,128)}) %reduce-scatter.9.cloned.1.call-update) | async-done | bytes 4194320 | tf_op jit(solution)/shard_map/reduce_scatter | solution.py:329
  1168.5 283.5 %reduce-scatter.11.cloned.1.call-done = f32[1024,1024]{1,0:T(8,128)} async-done(((f32[4096,1024]{1,0:T(8,128)}), f32[1024,1024]{1,0:T(8,128)}) %reduce-scatter.11.cloned.1.call-update) | async-done | bytes 4194320 | tf_op jit(solution)/shard_map/reduce_scatter | solution.py:331
  1455.1 49.1 %all-gather.6 = bf16[4,1,256]{2,1,0:T(2,128)(2,1)S(1)} all-gather(bf16[1,1,256]{2,1,0:T(2,128)(2,1)S(1)} %reshape.186), channel_id=1, replica_groups=mesh['rep'=8,'grp'=4] {'grp'}, dimensions={0}, use_global_device_ids=true | all-gather | bytes 2560 | tf_op jit(solution)/shard_map/all_gather | solution.py:297
  1523.9 10.3 fusion.67
  1534.2 17.8 %all-reduce.10 = (f32[1024]{0:T(1024)S(1)}, f32[1024]{0:T(1024)S(1)}, f32[2048]{0:T(1024)S(1)}, f32[1024]{0:T(1024)S(1)}, f32[1024]{0:T(1024)S(1)}, /*index=5*/f...) all-reduce(f32[1024]{0:T(1024)S(1)} %get-tuple-element.103, ...), channel_id=2, replica_groups=mesh['rep'=8,'grp'=4] {'grp'}, use_global_device_ids=true, to_apply=%region_16.17.clone | all-reduce | flops 12288 | bytes 98304
  1552.4 23.4 %all-reduce.8 = (f32[256]{0:T(256)}, f32[256]{0:T(256)}, f32[512]{0:T(512)}, f32[256]{0:T(256)}, f32[256]{0:T(256)}, /*index=5*/f32[256]{0:T(256)}, f32[1024]{0:T(1024)}, f32[256]{0:T(256)}) all-reduce(f32[256]{0:T(256)S(1)} %dynamic-slice.1, f32[256]{0:T(256)S(1)} %dynamic-slice.3, ...), channel_id=1, replica_groups=mesh['rep'=8,'grp'=4] {'rep'}, use_global_device_ids=true, to_apply=%region_17.18 | all-reduce | flops 3072 | bytes 24576 | tf_op jit(solution)/shard_map/psum | solution.py:334
  1581.2 9.9 fusion.79
  1591.1 38.0 %all-reduce.13.cloned.1.call-done = (f32[256,3072]{1,0:T(8,128)}, f32[256,1024]{1,0:T(8,128)}, f32[256,4096]{1,0:T(8,128)}, f32[1024,1024]{1,0:T(8,128)}) async-done(((f32[256,3072]{1,0:T(8,128)}, f32[256,1024]{1,0:T(8,128)}, f32[256,4096]{1,0:T(8,128)}, f32[1024,1024]{1,0:T(8,128)}), (f32[256,3072]{1,0:T(8,128)}, f32[256,1024]{1,0:T(8,128)}, f32[256,4096]{1,0:T(8,128)}, ...) | async-done | bytes 12582928 | tf_op jit(solution)/shard_map/psum | solution.py:334
  (252 shorter events, 182.7 us)
Async XLA Ops:
  7.2 120.9 %all-gather.12.cloned.1.call-start = ((), (), s32[]{:S(2)}) async-start(), calls=%async_computation.4 | async-start | bytes 7864320 | tf_op jit(solution)/shard_map/all_gather | solution.py:288
  7.9 15.0 copy-start.35
  7.9 23.1 %copy-start.32 = (bf16[512]{0:T(512)(128)(2,1)S(1)}, bf16[512]{0:T(512)(128)(2,1)}, u32[]{:S(2)}) copy-start(bf16[512]{0:T(512)(128)(2,1)} %param.23) | copy-start | bytes 3076
  7.9 165.6 %all-gather.14.cloned.1.call-start = ((), (), s32[]{:S(2)}) async-start(), calls=%async_computation.5 | async-start | bytes 2621440 | tf_op jit(solution)/shard_map/all_gather | solution.py:290
  8.7 314.9 %all-gather.16.cloned.1.call-start = ((), (), s32[]{:S(2)}) async-start(), calls=%async_computation.6 | async-start | bytes 10485760 | tf_op jit(solution)/shard_map/all_gather | solution.py:294
  9.4 463.4 %all-gather.18.cloned.1.call-start = ((), (), s32[]{:S(2)}) async-start(), calls=%async_computation.7 | async-start | bytes 10485760 | tf_op jit(solution)/shard_map/all_gather | solution.py:314
  10.0 23.4 %copy-start.36 = (bf16[256]{0:T(256)(128)(2,1)S(1)}, bf16[256]{0:T(256)(128)(2,1)}, u32[]{:S(2)}) copy-start(bf16[256]{0:T(256)(128)(2,1)} %param.25) | copy-start | bytes 1540
  10.0 35.3 %copy-start.37 = (bf16[256]{0:T(256)(128)(2,1)S(1)}, bf16[256]{0:T(256)(128)(2,1)}, u32[]{:S(2)}) copy-start(bf16[256]{0:T(256)(128)(2,1)} %param.26) | copy-start | bytes 1540
  10.0 43.5 %copy-start.31 = (bf16[1024]{0:T(1024)(128)(2,1)S(1)}, bf16[1024]{0:T(1024)(128)(2,1)}, u32[]{:S(2)}) copy-start(bf16[1024]{0:T(1024)(128)(2,1)} %param.29) | copy-start | bytes 6148
  10.0 62.0 %copy-start.38 = (bf16[256]{0:T(256)(128)(2,1)S(1)}, bf16[256]{0:T(256)(128)(2,1)}, u32[]{:S(2)}) copy-start(bf16[256]{0:T(256)(128)(2,1)} %param.27) | copy-start | bytes 1540
  10.0 94.7 %copy-start.4 = (bf16[1,577,1024]{2,1,0:T(8,128)(2,1)S(1)}, bf16[1,577,1024]{2,1,0:T(8,128)(2,1)}, u32[]{:S(2)}) copy-start(bf16[1,577,1024]{2,1,0:T(8,128)(2,1)} %param.18) | copy-start | bytes 3545092
  10.1 586.3 %reduce-scatter.7.cloned.1.call-start = ((), (), s32[]{:S(2)}) async-start(), calls=%async_computation.9 | async-start | bytes 5242880 | tf_op jit(solution)/shard_map/reduce_scatter | solution.py:325
  23.0 105.2 %copy-start.24 = (f32[4,1,256]{2,1,0:T(1,128)}, f32[4,1,256]{2,1,0:T(1,128)S(1)}, u32[]{:S(2)}) copy-start(f32[4,1,256]{2,1,0:T(1,128)S(1)} %convert_element_type.113) | copy-start | bytes 12292
  31.0 97.1 %copy-start.29 = (f32[4,1,256]{2,1,0:T(1,128)}, f32[4,1,256]{2,1,0:T(1,128)S(1)}, u32[]{:S(2)}) copy-start(f32[4,1,256]{2,1,0:T(1,128)S(1)} %convert_element_type.114) | copy-start | bytes 12292
  105.0 29.6 %copy-start.22 = (f32[577]{0:T(1024)}, f32[577]{0:T(1024)S(1)}, u32[]{:S(2)}) copy-start(f32[577]{0:T(1024)S(1)} %broadcast_multiply_fusion.5) | copy-start | bytes 6928
  105.5 29.2 %copy-start.26 = (f32[577]{0:T(1024)}, f32[577]{0:T(1024)S(1)}, u32[]{:S(2)}) copy-start(f32[577]{0:T(1024)S(1)} %add_rsqrt_fusion.1) | copy-start | bytes 6928
  472.8 13.1 copy-start.33
  505.4 379.7 %reduce-scatter.5.cloned.1.call-start = ((), (), s32[]{:S(2)}) async-start(), calls=%async_computation.8 | async-start | bytes 15728640 | tf_op jit(solution)/shard_map/reduce_scatter | solution.py:323
  564.6 603.9 %reduce-scatter.9.cloned.1.call-start = ((), (), s32[]{:S(2)}) async-start(), calls=%async_computation.10 | async-start | bytes 20971520 | tf_op jit(solution)/shard_map/reduce_scatter | solution.py:329
  579.5 872.4 %reduce-scatter.11.cloned.1.call-start = ((), (), s32[]{:S(2)}) async-start(), calls=%async_computation.11 | async-start | bytes 20971520 | tf_op jit(solution)/shard_map/reduce_scatter | solution.py:331
  592.4 1036.7 %all-reduce.13.cloned.1.call-start = ((), (), s32[]{:S(2)}) async-start(), calls=%async_computation.12 | async-start | bytes 25165824 | tf_op jit(solution)/shard_map/psum | solution.py:334
  592.5 859.5 %collective-permute-start = (bf16[1024,1024]{1,0:T(8,128)(2,1)}, bf16[1024,1024]{1,0:T(8,128)(2,1)}, u32[]{:S(2)}, u32[]{:S(2)}) collective-permute-start(bf16[1024,1024]{1,0:T(8,128)(2,1)} %param.30), channel_id=1, source_target_pairs={{0,1},{1,2},{2,3},{3,0},{4,5},{5,6},{6,7},{7,4},{8,9},{9,10},{10,1... | collective-permute-start | bytes 6291464 | tf_op jit(solution)/shard_map/ppermute | solution.py:22
  592.6 920.6 %collective-permute-start.1 = (bf16[1024,1024]{1,0:T(8,128)(2,1)}, bf16[1024,1024]{1,0:T(8,128)(2,1)}, u32[]{:S(2)}, u32[]{:S(2)}) collective-permute-start(bf16[1024,1024]{1,0:T(8,128)(2,1)} %param.30), channel_id=1, source_target_pairs={{0,3},{1,0},{2,1},{3,2},{4,7},{5,4},{6,5},{7,6},{8,11},{9,8},{10,9... | collective-permute-start | bytes 6291464 | tf_op jit(solution)/shard_map/ppermute | solution.py:27
  1452.0 64.3 %collective-permute-start.2 = (bf16[1024,1024]{1,0:T(8,128)(2,1)}, bf16[1024,1024]{1,0:T(8,128)(2,1)}, u32[]{:S(2)}, u32[]{:S(2)}) collective-permute-start(bf16[1024,1024]{1,0:T(8,128)(2,1)} %collective-permute-done), channel_id=1, source_target_pairs={{0,1},{1,2},{2,3},{3,0},{4,5},{5,6},{6,7},{7,4},{8,9},{9,10},{10,1... | collective-permute-start | bytes 6291464 | tf_op jit(solution)/shard_map/ppermute | solution.py:22
  (44 other events, 117.1 us)
Sparse Core Ops, SparseCore 0:
  9.6 118.4 all-gather.11
  129.7 43.7 all-gather.13
  175.1 148.4 all-gather.15
  325.0 147.7 all-gather.17
  505.6 74.9 reduce-scatter.6
  582.8 302.2 reduce-scatter.4
  887.5 280.9 reduce-scatter.8
  1170.8 281.0 reduce-scatter.10
  1455.9 173.1 all-reduce.12
